TPU v7x, 32 devices: a whole 2x2x4 slice. The times are simulated.
32 devices in a mesh: hour: 2 (over y), stn: 4 (over x, core), tchunk: 4 (over z).
Axes of the slice: x: 2, y: 2, z: 4, core: 2. Of those that a mesh axis runs over, the one named last changes fastest.
Arguments:
- raw_data: float32 [576, 32768], P('stn', ('hour', 'tchunk')), parts along dimension 1, may hold values from -500 to 500, as said below
- station_group: int32 [576], P('stn'), may hold values from 0 to 15
- partner_blocks: int32 [4, 3], P('stn'), may hold values from -1 to 3, as said below
Outputs:
- cross_spectra: float32 [8, 3, 512, 512], P(('hour', 'stn'), None, 'tchunk'), parts along dimension 0
There are 2 independent parts, one for each index of `hour`. A program takes and returns all parts, laid end to end along the dimension named above; an argument that names none is the same for every part. Nothing has to cross between parts.
Inputs may be any that keep to these rules, and one draw needn't show every extreme that they name: `raw_data`: recorded ground motion. `partner_blocks`: row b holds distinct blocks other than b in its first entries and -1 in the rest; every row has at least one partner and some row has 3.
All inputs are finite; a program needn't handle non-finite values.
Results may differ from a plain program's by a relative error of at most 0.0079.
Values may be sent and summed in bfloat16 or wider, within the bound.
A program may use at most 128 MiB of HBM per device.

v0:
```python
import functools
import math

import jax
import jax.numpy as jnp
import numpy as np
from jax import lax
from jax.experimental import pallas as pl
from jax.experimental.pallas import tpu as pltpu
from jax.sharding import PartitionSpec as P

SEGLEN = 4096
HOP = 2048
NBIN = 512
RB = 128
RAMH = 10
SMOOTH = 8
SUB = 16
MAXP = 3
PAD = 16
LANES = 128
VMEM_BYTES = 54000 * 1024

EPS_MEAN = 1e-06
LEVEL = 0.05
MESH = pl.DeviceIdType.MESH


def dft_table():
    sample = np.arange(SEGLEN)
    angles = (sample[:, None] * np.arange(1, NBIN + 1)[None, :] % SEGLEN) * (2.0 * math.pi / SEGLEN)
    taper = (0.5 - 0.5 * np.cos(sample * (2.0 * math.pi / SEGLEN)))[:, None]
    matrix = np.concatenate([taper * np.cos(angles), -taper * np.sin(angles)], axis=1)
    return jnp.asarray(matrix.astype(np.float32).astype(jnp.bfloat16))


def whiten(spectra, near):
    real_part = spectra[:, :NBIN]
    imag_part = spectra[:, NBIN:]
    powers = real_part * real_part + imag_part * imag_part
    bins = lax.broadcasted_iota(jnp.int32, (1, NBIN), 1)
    count = jnp.minimum(bins + SMOOTH, NBIN - 1) - jnp.maximum(bins - SMOOTH, 0) + 1
    high = powers.astype(jnp.bfloat16)
    rest = powers - high.astype(jnp.float32)
    middle = rest.astype(jnp.bfloat16)
    low = (rest - middle.astype(jnp.float32)).astype(jnp.bfloat16)
    total = (
        jnp.dot(high, near, preferred_element_type=jnp.float32)
        + jnp.dot(middle, near, preferred_element_type=jnp.float32)
        + jnp.dot(low, near, preferred_element_type=jnp.float32)
    )
    smooth = total * (1.0 / count.astype(jnp.float32))
    floor_level = jnp.sum(powers, axis=1, keepdims=True) * (1.0 / NBIN) + 1e-06
    scale = 1.0 / jnp.sqrt(smooth + LEVEL * floor_level)
    return jnp.concatenate([real_part * scale, imag_part * scale], axis=1).astype(jnp.bfloat16)


def spectra_kernel(
    slabs,
    groups,
    near_rows,
    raw_hbm,
    group_ref,
    partner_ref,
    table_hbm,
    out_ref,
    raw_ref,
    table,
    nearby,
    sums,
    halo,
    norm,
    from_next,
    from_prev,
    outbox,
    inbox,
    spread_whole,
    spread_split,
    gathered_whole,
    gathered_split,
    mine,
    other,
    raw_sem,
    table_sem,
    sum_send,
    sum_recv,
    hop_send,
    hop_recv,
    mix_send,
    mix_recv,
    all_send,
    all_recv,
):
    stations, samples = raw_ref.shape
    blocks = samples // RB
    bins = NBIN // slabs
    t = lax.axis_index("tchunk")
    b = lax.axis_index("stn")
    has_next = t < slabs - 1
    has_prev = t > 0
    nxt = jnp.minimum(t + 1, slabs - 1)
    prv = jnp.maximum(t - 1, 0)

    chunk = samples // 4
    loads = []
    for part in range(4):
        columns = slice(part * chunk, (part + 1) * chunk)
        load = pltpu.make_async_copy(
            raw_hbm.at[:, columns], raw_ref.at[:, columns], raw_sem.at[part]
        )
        load.start()
        loads.append(load)
    fetch = pltpu.make_async_copy(table_hbm, table, table_sem)

    barrier = pltpu.get_barrier_semaphore()
    for step in range(1, slabs):
        pl.semaphore_signal(
            barrier, inc=1, device_id={"tchunk": lax.rem(t + step, slabs)}, device_id_type=MESH
        )
    for step in range(1, groups):
        pl.semaphore_signal(
            barrier, inc=1, device_id={"stn": lax.rem(b + step, groups)}, device_id_type=MESH
        )

    wide = sums.shape[1]
    lane = lax.broadcasted_iota(jnp.int32, (stations, LANES), 1)
    acc = jnp.zeros((stations, LANES), jnp.float32)
    for block in range(blocks):
        if block * RB % chunk == 0:
            loads[block * RB // chunk].wait()
            if block * RB // chunk == len(loads) - 1:
                fetch.start()
        part = jnp.sum(jnp.abs(raw_ref[:, block * RB : (block + 1) * RB]), axis=1, keepdims=True)
        acc = jnp.where(lane == block, part, acc)
    tall = jnp.concatenate([acc, jnp.zeros((wide - stations, LANES), jnp.float32)], axis=0)
    sums[0:PAD, :] = jnp.zeros((PAD, wide), jnp.float32)
    sums[PAD : PAD + blocks, :] = tall.T[:blocks, :]
    sums[PAD + blocks : 2 * PAD + blocks, :] = jnp.zeros((PAD, wide), jnp.float32)

    pl.semaphore_wait(barrier, slabs - 1 + groups - 1)

    def remote(source, target, sends, recvs, index, place):
        return pltpu.make_async_remote_copy(
            src_ref=source,
            dst_ref=target,
            send_sem=sends.at[index],
            recv_sem=recvs.at[index],
            device_id=place,
            device_id_type=MESH,
        )

    up = {"tchunk": nxt}
    down = {"tchunk": prv}
    sums_up = remote(sums.at[blocks : blocks + PAD, :], halo.at[0], sum_send, sum_recv, 0, up)
    sums_down = remote(sums.at[PAD : 2 * PAD, :], halo.at[1], sum_send, sum_recv, 1, down)

    @pl.when(has_next)
    def _():
        sums_up.start()

    @pl.when(has_prev)
    def _():
        sums_down.start()

    def inverses():
        window = sums[PAD - RAMH : PAD - RAMH + blocks, :]
        for offset in range(1, 2 * RAMH):
            window = window + sums[PAD - RAMH + offset : PAD - RAMH + offset + blocks, :]
        here = t * blocks + lax.broadcasted_iota(jnp.int32, (blocks, wide), 0)
        counted = jnp.minimum(here + RAMH, blocks * slabs) - jnp.maximum(here - RAMH, 0)
        running = window / (RB * counted.astype(jnp.float32))
        inverse = 1.0 / (running + EPS_MEAN)
        return jnp.concatenate(
            [inverse, jnp.zeros((LANES - blocks, wide), jnp.float32)], axis=0
        ).T[:stations, :]

    def normalize(inverse, chosen):
        for block in chosen:
            columns = slice(block * RB, (block + 1) * RB)
            norm[:, columns] = (raw_ref[:, columns] * inverse[:, block : block + 1]).astype(
                jnp.bfloat16
            )

    first, last = RAMH, blocks - RAMH + 1
    normalize(inverses(), range(first, last))
    cut_down = first * RB
    cut_up = last * RB - HOP

    def hop_copies():
        return (
            remote(
                norm.at[0:near_rows, cut_down:HOP],
                from_next.at[:, cut_down:HOP],
                hop_send, hop_recv, 0, down,
            ),
            remote(
                norm.at[near_rows:stations, HOP : HOP + cut_up],
                from_prev.at[:, 0:cut_up],
                hop_send, hop_recv, 1, up,
            ),
            remote(
                norm.at[0:near_rows, 0:cut_down],
                from_next.at[:, 0:cut_down],
                hop_send, hop_recv, 2, down,
            ),
            remote(
                norm.at[near_rows:stations, HOP + cut_up : 2 * HOP],
                from_prev.at[:, cut_up:HOP],
                hop_send, hop_recv, 3, up,
            ),
        )

    down_early, up_early, down_late, up_late = hop_copies()

    @pl.when(has_prev)
    def _():
        down_early.start()

    @pl.when(has_next)
    def _():
        up_early.start()

    @pl.when(jnp.logical_not(has_prev))
    def _():
        from_prev[...] = jnp.zeros_like(from_prev)

    @pl.when(jnp.logical_not(has_next))
    def _():
        from_next[...] = jnp.zeros_like(from_next)

    @pl.when(has_prev)
    def _():
        sums_up.wait_recv()
        sums[0:PAD, :] = halo[0]

    @pl.when(has_next)
    def _():
        sums_down.wait_recv()
        sums[PAD + blocks : 2 * PAD + blocks, :] = halo[1]

    normalize(inverses(), [*range(first), *range(last, blocks)])

    @pl.when(has_prev)
    def _():
        down_late.start()

    @pl.when(has_next)
    def _():
        up_late.start()

    row = lax.broadcasted_iota(jnp.int32, (NBIN, NBIN), 0)
    col = lax.broadcasted_iota(jnp.int32, (NBIN, NBIN), 1)
    nearby[...] = (jnp.abs(row - col) <= SMOOTH).astype(jnp.float32).astype(jnp.bfloat16)
    member = (
        group_ref[...] == lax.broadcasted_iota(jnp.int32, (SUB, stations), 0)
    ).astype(jnp.float32)

    def put_beams(piece, spectra, members):
        sums_here = jnp.dot(
            members.astype(jnp.bfloat16),
            whiten(spectra, nearby[...]),
            preferred_element_type=jnp.float32,
        ).astype(jnp.bfloat16)
        for part in range(2):
            for slab in range(slabs):
                begin = part * NBIN + slab * bins
                outbox[piece, slab, part] = sums_here[:, begin : begin + bins]
        copies = []
        for step in range(1, slabs):
            to = lax.rem(t + step, slabs)
            copy = remote(
                outbox.at[piece, to],
                inbox.at[piece, t],
                mix_send,
                mix_recv,
                piece * (slabs - 1) + step - 1,
                {"tchunk": to},
            )
            copy.start()
            copies.append(copy)
        inbox[piece, t] = outbox[piece, t]
        return copies

    spreads = (spread_whole, spread_split)
    gathers = (gathered_whole, gathered_split)

    def share(half):
        copies = []
        for step in range(1, groups):
            copy = remote(
                spreads[half],
                gathers[half].at[b],
                all_send,
                all_recv,
                half * (groups - 1) + step - 1,
                {"stn": lax.rem(b + step, groups)},
            )
            copy.start()
            copies.append(copy)
        gathers[half][b] = spreads[half][...]
        return copies

    pairs = SUB * SUB
    pair_row = lax.broadcasted_iota(jnp.int32, (SUB, pairs), 0)
    pair_col = lax.broadcasted_iota(jnp.int32, (SUB, pairs), 1)
    left_hot = (pair_col // SUB == pair_row).astype(jnp.float32).astype(jnp.bfloat16)
    right_hot = (pair_col % SUB == pair_row).astype(jnp.float32).astype(jnp.bfloat16)

    def expand(beams, hot):
        return lax.dot_general(
            beams, hot, (((0,), (0,)), ((), ())), preferred_element_type=jnp.float32
        )

    def expand_mine(half):
        for index in range(spreads[half].shape[0]):
            mine[index] = expand(spreads[half][index], left_hot)

    def stack(half):
        count = spreads[half].shape[0]
        tile = 8
        for slot in range(MAXP):
            partner = partner_ref[0, slot]
            chosen = jnp.maximum(partner, 0)
            weight = jnp.where(partner >= 0, 1.0 / (2 * slabs - 1), 0.0)
            for index in range(count):
                other[slot, index] = expand(gathers[half][chosen, index], right_hot)

            @pl.loop(0, bins // tile)
            def _(step):
                rows = pl.ds(pl.multiple_of(step * tile, tile), tile)
                if half == 0:
                    real_sum = jnp.zeros((tile, pairs), jnp.float32)
                    imag_sum = jnp.zeros((tile, pairs), jnp.float32)
                else:
                    real_sum = out_ref[0, slot, rows, 0:pairs]
                    imag_sum = out_ref[0, slot, rows, pairs : 2 * pairs]
                for segment in range(count // 2):
                    a = mine[2 * segment, rows]
                    c = mine[2 * segment + 1, rows]
                    d = other[slot, 2 * segment, rows]
                    e = other[slot, 2 * segment + 1, rows]
                    real_sum = real_sum + a * d + c * e
                    imag_sum = imag_sum + c * d - a * e
                if half == 1:
                    real_sum = real_sum * weight
                    imag_sum = imag_sum * weight
                out_ref[0, slot, rows, 0:pairs] = real_sum
                out_ref[0, slot, rows, pairs : 2 * pairs] = imag_sum

    def dot(left, right):
        return jnp.dot(left, right, preferred_element_type=jnp.float32)

    fetch.wait()
    low = dot(jnp.concatenate([norm[:, :HOP], norm[0:near_rows, HOP:]], axis=0), table[:HOP])
    high = dot(jnp.concatenate([norm[:, HOP:], norm[near_rows:, :HOP]], axis=0), table[HOP:])
    mixes = put_beams(0, low[:stations] + high[:stations], member)
    near = low[stations:]
    far = high[stations:]

    @pl.when(has_next)
    def _():
        down_early.wait_recv()

    @pl.when(has_prev)
    def _():
        up_early.wait_recv()

    far = far + dot(from_prev[:, :cut_up], table[:cut_up])
    near = near + dot(from_next[:, cut_down:], table[HOP + cut_down :])

    @pl.when(has_prev)
    def _():
        up_late.wait_recv()

    far = far + dot(from_prev[:, cut_up:], table[cut_up:HOP])
    far_mixes = put_beams(2, far, member[:, near_rows:])

    @pl.when(has_next)
    def _():
        down_late.wait_recv()

    near = near + dot(from_next[:, :cut_down], table[HOP : HOP + cut_down])
    near_mixes = put_beams(1, near, member[:, :near_rows])

    for copy in mixes:
        copy.wait()
    for slab in range(slabs):
        for part in range(2):
            spread_whole[2 * slab + part] = inbox[0, slab, part]
    whole_shares = share(0)
    expand_mine(0)

    for copy in [*far_mixes, *near_mixes]:
        copy.wait()
    for slab in range(slabs - 1):
        for part in range(2):
            both = inbox[1, slab, part].astype(jnp.float32)
            both = both + inbox[2, slab + 1, part].astype(jnp.float32)
            spread_split[2 * slab + part] = both.astype(jnp.bfloat16)
    split_shares = share(1)

    for copy in whole_shares:
        copy.wait()
    stack(0)
    expand_mine(1)

    @pl.when(has_next)
    def _():
        sums_up.wait_send()
        up_early.wait_send()
        up_late.wait_send()

    @pl.when(has_prev)
    def _():
        sums_down.wait_send()
        down_early.wait_send()
        down_late.wait_send()

    for copy in split_shares:
        copy.wait()
    stack(1)


def body(raw_data, station_group, partner_blocks):
    stations, samples = raw_data.shape
    slabs = lax.axis_size("tchunk")
    groups = lax.axis_size("stn")
    bins = NBIN // slabs
    blocks = samples // RB
    near_rows = -(-stations // 32) * 16
    wide = -(-stations // LANES) * LANES
    vmem = pl.BlockSpec(memory_space=pltpu.VMEM)
    dma = pltpu.SemaphoreType.DMA
    pairs = SUB * SUB
    whole_shape = (2 * slabs, SUB, bins)
    split_shape = (2 * slabs - 2, SUB, bins)
    far = pl.BlockSpec(memory_space=pltpu.HBM)
    return pl.pallas_call(
        functools.partial(spectra_kernel, slabs, groups, near_rows),
        out_shape=jax.ShapeDtypeStruct((1, MAXP, bins, 2 * pairs), jnp.float32),
        in_specs=[far, vmem, pl.BlockSpec(memory_space=pltpu.SMEM), far],
        out_specs=vmem,
        scratch_shapes=[
            pltpu.VMEM((stations, samples), jnp.float32),
            pltpu.VMEM((SEGLEN, 2 * NBIN), jnp.bfloat16),
            pltpu.VMEM((NBIN, NBIN), jnp.bfloat16),
            pltpu.VMEM((2 * PAD + blocks, wide), jnp.float32),
            pltpu.VMEM((2, PAD, wide), jnp.float32),
            pltpu.VMEM((stations, samples), jnp.bfloat16),
            pltpu.VMEM((near_rows, HOP), jnp.bfloat16),
            pltpu.VMEM((stations - near_rows, HOP), jnp.bfloat16),
            pltpu.VMEM((3, slabs, 2, SUB, bins), jnp.bfloat16),
            pltpu.VMEM((3, slabs, 2, SUB, bins), jnp.bfloat16),
            pltpu.VMEM(whole_shape, jnp.bfloat16),
            pltpu.VMEM(split_shape, jnp.bfloat16),
            pltpu.VMEM((groups,) + whole_shape, jnp.bfloat16),
            pltpu.VMEM((groups,) + split_shape, jnp.bfloat16),
            pltpu.VMEM((2 * slabs, bins, pairs), jnp.float32),
            pltpu.VMEM((MAXP, 2 * slabs, bins, pairs), jnp.float32),
            dma((4,)),
            dma,
            dma((2,)),
            dma((2,)),
            dma((4,)),
            dma((4,)),
            dma((3 * (slabs - 1),)),
            dma((3 * (slabs - 1),)),
            dma((2 * (groups - 1),)),
            dma((2 * (groups - 1),)),
        ],
        compiler_params=pltpu.CompilerParams(
            collective_id=0, has_side_effects=True, vmem_limit_bytes=VMEM_BYTES
        ),
    )(raw_data, station_group[None, :], partner_blocks, dft_table())


def solution(mesh):
    placed = (P("stn", ("hour", "tchunk")), P("stn"), P("stn", None))
    return jax.shard_map(
        body,
        mesh=mesh,
        in_specs=placed,
        out_specs=P(("hour", "stn"), None, "tchunk", None),
        check_vma=False,
    )
```

profile of v0, /device:TPU:0, one launch (start us, length us, event | category | flops | bytes accessed | tf_op | source)
XLA Modules:
  0.0 27.4 jit_solution(7460252914253796582)
XLA Ops:
  0.0 0.0 copy-start
  0.0 0.7 %copy-done = s32[144]{0:T(256)S(1)} copy-done((s32[144]{0:T(256)S(1)}, s32[144]{0:T(256)}, u32[]{:S(2)}) %copy-start) | copy-done | bytes 600
  0.7 0.0 copy-start.1
  0.7 0.7 %copy-done.1 = s32[1,3]{1,0:T(1,128)S(1)} copy-done((s32[1,3]{1,0:T(1,128)S(1)}, s32[1,3]{1,0:T(1,128)}, u32[]{:S(2)}) %copy-start.1) | copy-done | bytes 36
  1.3 25.2 %shard_map.46 = f32[1,3,128,512]{3,2,1,0:T(8,128)S(1)} custom-call(f32[144,4096]{1,0:T(8,128)} %raw_hbm.1, s32[1,144]{1,0:T(1,128)S(1)} %bitcast.1, s32[1,3]{1,0:T(1,128)S(1)} %copy-done.1, bf16[4096,1024]{1,0:T(8,128)(2,1)} %constant.2.clone.table_hbm), custom_call_target="tpu_custom_call" | custom-call | tf_op jit(solution)/shard_map/pallas_call | solution.py:438
  26.6 0.9 %copy.6 = f32[1,3,128,512]{3,2,1,0:T(8,128)} copy(f32[1,3,128,512]{3,2,1,0:T(8,128)S(1)} %shard_map.46) | data formatting | bytes 1572864
Async XLA Ops:
  0.0 0.7 %copy-start = (s32[144]{0:T(256)S(1)}, s32[144]{0:T(256)}, u32[]{:S(2)}) copy-start(s32[144]{0:T(256)} %param.5) | copy-start | bytes 1732
  0.7 0.7 %copy-start.1 = (s32[1,3]{1,0:T(1,128)S(1)}, s32[1,3]{1,0:T(1,128)}, u32[]{:S(2)}) copy-start(s32[1,3]{1,0:T(1,128)} %partner_ref.1) | copy-start | bytes 40
where the time goes:
time: 27.6 us; the launch traced here: 27.4 us
  Pallas kernels  25.2 us (91%)
  local copies, waits for them, and re-layouts  2.22 us (8%)
    pallas_call x1, Pallas kernels, body(): pl.pallas_call(functools.partial(spectra_kernel, slabs, groups, near_rows...  25.2 us
    unnamed x5, local copies, waits for them, and re-layouts  2.22 us

commit v1 on v0

--- a/solution.py
+++ b/solution.py
@@ -19,6 +19,8 @@
 MAXP = 3
 PAD = 16
 LANES = 128
+CHUNK = 2 * LANES
+CHUNKS = 2 * NBIN // CHUNK
 VMEM_BYTES = 54000 * 1024
 
 EPS_MEAN = 1e-06
@@ -30,28 +32,27 @@
     sample = np.arange(SEGLEN)
     angles = (sample[:, None] * np.arange(1, NBIN + 1)[None, :] % SEGLEN) * (2.0 * math.pi / SEGLEN)
     taper = (0.5 - 0.5 * np.cos(sample * (2.0 * math.pi / SEGLEN)))[:, None]
-    matrix = np.concatenate([taper * np.cos(angles), -taper * np.sin(angles)], axis=1)
+    parts = np.stack([taper * np.cos(angles), -taper * np.sin(angles)])
+    parts = parts.reshape(2, 2, HOP, CHUNKS, LANES).transpose(1, 3, 2, 0, 4)
+    matrix = parts.reshape(2, CHUNKS, HOP, CHUNK)
     return jnp.asarray(matrix.astype(np.float32).astype(jnp.bfloat16))
 
 
 def whiten(spectra, near):
-    real_part = spectra[:, :NBIN]
-    imag_part = spectra[:, NBIN:]
+    starts = range(0, 2 * NBIN, CHUNK)
+    real_part = jnp.concatenate([spectra[:, at : at + LANES] for at in starts], axis=1)
+    imag_part = jnp.concatenate([spectra[:, at + LANES : at + CHUNK] for at in starts], axis=1)
     powers = real_part * real_part + imag_part * imag_part
     bins = lax.broadcasted_iota(jnp.int32, (1, NBIN), 1)
     count = jnp.minimum(bins + SMOOTH, NBIN - 1) - jnp.maximum(bins - SMOOTH, 0) + 1
     high = powers.astype(jnp.bfloat16)
-    rest = powers - high.astype(jnp.float32)
-    middle = rest.astype(jnp.bfloat16)
-    low = (rest - middle.astype(jnp.float32)).astype(jnp.bfloat16)
-    total = (
-        jnp.dot(high, near, preferred_element_type=jnp.float32)
-        + jnp.dot(middle, near, preferred_element_type=jnp.float32)
-        + jnp.dot(low, near, preferred_element_type=jnp.float32)
+    rest = (powers - high.astype(jnp.float32)).astype(jnp.bfloat16)
+    total = jnp.dot(high, near, preferred_element_type=jnp.float32) + jnp.dot(
+        rest, near, preferred_element_type=jnp.float32
     )
     smooth = total * (1.0 / count.astype(jnp.float32))
     floor_level = jnp.sum(powers, axis=1, keepdims=True) * (1.0 / NBIN) + 1e-06
-    scale = 1.0 / jnp.sqrt(smooth + LEVEL * floor_level)
+    scale = lax.rsqrt(smooth + LEVEL * floor_level)
     return jnp.concatenate([real_part * scale, imag_part * scale], axis=1).astype(jnp.bfloat16)
 
 
@@ -60,18 +61,24 @@
     groups,
     near_rows,
     raw_hbm,
-    group_ref,
-    partner_ref,
+    group_hbm,
+    partner_hbm,
     table_hbm,
     out_ref,
     raw_ref,
+    group_ref,
+    partner_ref,
     table,
     nearby,
     sums,
     halo,
     norm,
-    from_next,
-    from_prev,
+    own,
+    keep,
+    near_out,
+    far_out,
+    near_in,
+    far_in,
     outbox,
     inbox,
     spread_whole,
@@ -82,6 +89,7 @@
     other,
     raw_sem,
     table_sem,
+    argument_sem,
     sum_send,
     sum_recv,
     hop_send,
@@ -110,7 +118,24 @@
         )
         load.start()
         loads.append(load)
-    fetch = pltpu.make_async_copy(table_hbm, table, table_sem)
+    fetches = [
+        [
+            pltpu.make_async_copy(
+                table_hbm.at[side, part], table.at[side, part], table_sem.at[side, part]
+            )
+            for part in range(CHUNKS)
+        ]
+        for side in range(2)
+    ]
+    argument_loads = (
+        pltpu.make_async_copy(group_hbm, group_ref, argument_sem.at[0]),
+        pltpu.make_async_copy(partner_hbm, partner_ref, argument_sem.at[1]),
+    )
+    for load in argument_loads:
+        load.start()
+    for part in range(CHUNKS):
+        for side in range(2):
+            fetches[side][part].start()
 
     barrier = pltpu.get_barrier_semaphore()
     for step in range(1, slabs):
@@ -128,8 +153,6 @@
     for block in range(blocks):
         if block * RB % chunk == 0:
             loads[block * RB // chunk].wait()
-            if block * RB // chunk == len(loads) - 1:
-                fetch.start()
         part = jnp.sum(jnp.abs(raw_ref[:, block * RB : (block + 1) * RB]), axis=1, keepdims=True)
         acc = jnp.where(lane == block, part, acc)
     tall = jnp.concatenate([acc, jnp.zeros((wide - stations, LANES), jnp.float32)], axis=0)
@@ -183,50 +206,14 @@
 
     first, last = RAMH, blocks - RAMH + 1
     normalize(inverses(), range(first, last))
-    cut_down = first * RB
-    cut_up = last * RB - HOP
-
-    def hop_copies():
-        return (
-            remote(
-                norm.at[0:near_rows, cut_down:HOP],
-                from_next.at[:, cut_down:HOP],
-                hop_send, hop_recv, 0, down,
-            ),
-            remote(
-                norm.at[near_rows:stations, HOP : HOP + cut_up],
-                from_prev.at[:, 0:cut_up],
-                hop_send, hop_recv, 1, up,
-            ),
-            remote(
-                norm.at[0:near_rows, 0:cut_down],
-                from_next.at[:, 0:cut_down],
-                hop_send, hop_recv, 2, down,
-            ),
-            remote(
-                norm.at[near_rows:stations, HOP + cut_up : 2 * HOP],
-                from_prev.at[:, cut_up:HOP],
-                hop_send, hop_recv, 3, up,
-            ),
-        )
-
-    down_early, up_early, down_late, up_late = hop_copies()
-
-    @pl.when(has_prev)
-    def _():
-        down_early.start()
-
-    @pl.when(has_next)
-    def _():
-        up_early.start()
 
     @pl.when(jnp.logical_not(has_prev))
     def _():
-        from_prev[...] = jnp.zeros_like(from_prev)
+        far_in[...] = jnp.zeros_like(far_in)
 
     @pl.when(jnp.logical_not(has_next))
     def _():
-        from_next[...] = jnp.zeros_like(from_next)
+        near_in[...] = jnp.zeros_like(near_in)
 
     @pl.when(has_prev)
     def _():
@@ -239,46 +226,44 @@
         sums[PAD + blocks : 2 * PAD + blocks, :] = halo[1]
 
     normalize(inverses(), [*range(first), *range(last, blocks)])
-
-    @pl.when(has_prev)
-    def _():
-        down_late.start()
-
-    @pl.when(has_next)
-    def _():
-        up_late.start()
 
     row = lax.broadcasted_iota(jnp.int32, (NBIN, NBIN), 0)
     col = lax.broadcasted_iota(jnp.int32, (NBIN, NBIN), 1)
     nearby[...] = (jnp.abs(row - col) <= SMOOTH).astype(jnp.float32).astype(jnp.bfloat16)
+    for load in argument_loads:
+        load.wait()
     member = (
         group_ref[...] == lax.broadcasted_iota(jnp.int32, (SUB, stations), 0)
     ).astype(jnp.float32)
 
-    def put_beams(piece, spectra, members):
+    def put_beams(pieces, spectra, members):
         sums_here = jnp.dot(
             members.astype(jnp.bfloat16),
             whiten(spectra, nearby[...]),
             preferred_element_type=jnp.float32,
         ).astype(jnp.bfloat16)
-        for part in range(2):
-            for slab in range(slabs):
-                begin = part * NBIN + slab * bins
-                outbox[piece, slab, part] = sums_here[:, begin : begin + bins]
+        for index, piece in enumerate(pieces):
+            rows = slice(index * SUB, (index + 1) * SUB)
+            for part in range(2):
+                for slab in range(slabs):
+                    begin = part * NBIN + slab * bins
+                    outbox[piece, slab, part] = sums_here[rows, begin : begin + bins]
         copies = []
-        for step in range(1, slabs):
+        for step in range(slabs - 1, 0, -1):
             to = lax.rem(t + step, slabs)
-            copy = remote(
-                outbox.at[piece, to],
-                inbox.at[piece, t],
-                mix_send,
-                mix_recv,
-                piece * (slabs - 1) + step - 1,
-                {"tchunk": to},
-            )
-            copy.start()
-            copies.append(copy)
-        inbox[piece, t] = outbox[piece, t]
+            for piece in pieces:
+                copy = remote(
+                    outbox.at[piece, to],
+                    inbox.at[piece, t],
+                    mix_send,
+                    mix_recv,
+                    piece * (slabs - 1) + step - 1,
+                    {"tchunk": to},
+                )
+                copy.start()
+                copies.append(copy)
+        for piece in pieces:
+            inbox[piece, t] = outbox[piece, t]
         return copies
 
     spreads = (spread_whole, spread_split)
@@ -350,37 +335,50 @@
     def dot(left, right):
         return jnp.dot(left, right, preferred_element_type=jnp.float32)
 
-    fetch.wait()
-    low = dot(jnp.concatenate([norm[:, :HOP], norm[0:near_rows, HOP:]], axis=0), table[:HOP])
-    high = dot(jnp.concatenate([norm[:, HOP:], norm[near_rows:, :HOP]], axis=0), table[HOP:])
-    mixes = put_beams(0, low[:stations] + high[:stations], member)
-    near = low[stations:]
-    far = high[stations:]
+    near_copies = []
+    far_copies = []
+    for part in range(CHUNKS):
+        columns = slice(part * CHUNK, (part + 1) * CHUNK)
+        fetches[0][part].wait()
+        opening = dot(norm[:, HOP:], table[0, part])
+        far_out[part] = opening[near_rows:].astype(jnp.bfloat16)
+        keep[:near_rows, columns] = opening[:near_rows]
+        far_copies.append(remote(far_out.at[part], far_in.at[part], hop_send, hop_recv, part, up))
+        pl.when(has_next)(far_copies[-1].start)
+        fetches[1][part].wait()
+        closing = dot(norm[:, :HOP], table[1, part])
+        near_out[part] = closing[:near_rows].astype(jnp.bfloat16)
+        keep[near_rows:, columns] = closing[near_rows:]
+        near_copies.append(
+            remote(near_out.at[part], near_in.at[part], hop_send, hop_recv, CHUNKS + part, down)
+        )
+        pl.when(has_prev)(near_copies[-1].start)
+
+    for part in range(CHUNKS):
+        columns = slice(part * CHUNK, (part + 1) * CHUNK)
+        own[:, columns] = dot(norm[:, :HOP], table[0, part]) + dot(norm[:, HOP:], table[1, part])
+    mixes = put_beams((0,), own[...], member)
 
     @pl.when(has_next)
     def _():
-        down_early.wait_recv()
+        for copy in near_copies:
+            copy.wait_recv()
 
     @pl.when(has_prev)
     def _():
-        up_early.wait_recv()
-
-    far = far + dot(from_prev[:, :cut_up], table[:cut_up])
-    near = near + dot(from_next[:, cut_down:], table[HOP + cut_down :])
-
-    @pl.when(has_prev)
-    def _():
-        up_late.wait_recv()
-
-    far = far + dot(from_prev[:, cut_up:], table[cut_up:HOP])
-    far_mixes = put_beams(2, far, member[:, near_rows:])
-
-    @pl.when(has_next)
-    def _():
-        down_late.wait_recv()
-
-    near = near + dot(from_next[:, :cut_down], table[HOP : HOP + cut_down])
-    near_mixes = put_beams(1, near, member[:, :near_rows])
+        for copy in far_copies:
+            copy.wait_recv()
+
+    for part in range(CHUNKS):
+        columns = slice(part * CHUNK, (part + 1) * CHUNK)
+        own[:near_rows, columns] = keep[:near_rows, columns] + near_in[part].astype(jnp.float32)
+        own[near_rows:, columns] = keep[near_rows:, columns] + far_in[part].astype(jnp.float32)
+    station = lax.broadcasted_iota(jnp.int32, (SUB, stations), 1)
+    split_member = jnp.concatenate(
+        [jnp.where(station < near_rows, member, 0.0), jnp.where(station < near_rows, 0.0, member)],
+        axis=0,
+    )
+    split_mixes = put_beams((1, 2), own[...], split_member)
 
     for copy in mixes:
         copy.wait()
@@ -390,7 +388,7 @@
     whole_shares = share(0)
     expand_mine(0)
 
-    for copy in [*far_mixes, *near_mixes]:
+    for copy in split_mixes:
         copy.wait()
     for slab in range(slabs - 1):
         for part in range(2):
@@ -407,14 +405,14 @@
     @pl.when(has_next)
     def _():
         sums_up.wait_send()
-        up_early.wait_send()
-        up_late.wait_send()
+        for copy in far_copies:
+            copy.wait_send()
 
     @pl.when(has_prev)
     def _():
         sums_down.wait_send()
-        down_early.wait_send()
-        down_late.wait_send()
+        for copy in near_copies:
+            copy.wait_send()
 
     for copy in split_shares:
         copy.wait()
@@ -438,17 +436,23 @@
     return pl.pallas_call(
         functools.partial(spectra_kernel, slabs, groups, near_rows),
         out_shape=jax.ShapeDtypeStruct((1, MAXP, bins, 2 * pairs), jnp.float32),
-        in_specs=[far, vmem, pl.BlockSpec(memory_space=pltpu.SMEM), far],
+        in_specs=[far, far, far, far],
         out_specs=vmem,
         scratch_shapes=[
             pltpu.VMEM((stations, samples), jnp.float32),
-            pltpu.VMEM((SEGLEN, 2 * NBIN), jnp.bfloat16),
+            pltpu.VMEM((1, stations), jnp.int32),
+            pltpu.SMEM((1, MAXP), jnp.int32),
+            pltpu.VMEM((2, CHUNKS, HOP, CHUNK), jnp.bfloat16),
             pltpu.VMEM((NBIN, NBIN), jnp.bfloat16),
             pltpu.VMEM((2 * PAD + blocks, wide), jnp.float32),
             pltpu.VMEM((2, PAD, wide), jnp.float32),
             pltpu.VMEM((stations, samples), jnp.bfloat16),
-            pltpu.VMEM((near_rows, HOP), jnp.bfloat16),
-            pltpu.VMEM((stations - near_rows, HOP), jnp.bfloat16),
+            pltpu.VMEM((stations, 2 * NBIN), jnp.float32),
+            pltpu.VMEM((stations, 2 * NBIN), jnp.float32),
+            pltpu.VMEM((CHUNKS, near_rows, CHUNK), jnp.bfloat16),
+            pltpu.VMEM((CHUNKS, stations - near_rows, CHUNK), jnp.bfloat16),
+            pltpu.VMEM((CHUNKS, near_rows, CHUNK), jnp.bfloat16),
+            pltpu.VMEM((CHUNKS, stations - near_rows, CHUNK), jnp.bfloat16),
             pltpu.VMEM((3, slabs, 2, SUB, bins), jnp.bfloat16),
             pltpu.VMEM((3, slabs, 2, SUB, bins), jnp.bfloat16),
             pltpu.VMEM(whole_shape, jnp.bfloat16),
@@ -458,11 +462,12 @@
             pltpu.VMEM((2 * slabs, bins, pairs), jnp.float32),
             pltpu.VMEM((MAXP, 2 * slabs, bins, pairs), jnp.float32),
             dma((4,)),
-            dma,
+            dma((2, CHUNKS)),
             dma((2,)),
             dma((2,)),
-            dma((4,)),
-            dma((4,)),
+            dma((2,)),
+            dma((2 * CHUNKS,)),
+            dma((2 * CHUNKS,)),
             dma((3 * (slabs - 1),)),
             dma((3 * (slabs - 1),)),
             dma((2 * (groups - 1),)),

time: 27.6 us -> 27.5 us (level)
  no operation moved by 1% of the time
where the time goes in v1:
time: 27.5 us; the launch traced here: 27.3 us
  Pallas kernels  25.1 us (91%)
  local copies, waits for them, and re-layouts  2.22 us (8%)
    pallas_call x1, Pallas kernels, body(): pl.pallas_call(functools.partial(spectra_kernel, slabs, groups, near_rows...  25.1 us
    unnamed x5, local copies, waits for them, and re-layouts  2.22 us

profile of v1, /device:TPU:0, one launch (start us, length us, event | category | flops | bytes accessed | tf_op | source)
XLA Modules:
  0.0 27.3 jit_solution(4835221617118810481)
XLA Ops:
  0.0 0.0 copy-start
  0.0 0.7 %copy-done = s32[144]{0:T(256)S(1)} copy-done((s32[144]{0:T(256)S(1)}, s32[144]{0:T(256)}, u32[]{:S(2)}) %copy-start) | copy-done | bytes 600
  0.7 0.0 copy-start.1
  0.7 0.7 %copy-done.1 = s32[1,3]{1,0:T(1,128)S(1)} copy-done((s32[1,3]{1,0:T(1,128)S(1)}, s32[1,3]{1,0:T(1,128)}, u32[]{:S(2)}) %copy-start.1) | copy-done | bytes 36
  1.3 25.1 %shard_map.46 = f32[1,3,128,512]{3,2,1,0:T(8,128)S(1)} custom-call(f32[144,4096]{1,0:T(8,128)} %raw_hbm.1, s32[1,144]{1,0:T(1,128)S(1)} %bitcast.1, s32[1,3]{1,0:T(1,128)S(1)} %copy-done.1, bf16[2,4,2048,256]{3,2,1,0:T(8,128)(2,1)} %constant.2.clone.table_hbm), custom_call_target="tpu_custom_call" | custom-call | tf_op jit(solution)/shard_map/pallas_call | solution.py:436
  26.4 0.9 %copy.6 = f32[1,3,128,512]{3,2,1,0:T(8,128)} copy(f32[1,3,128,512]{3,2,1,0:T(8,128)S(1)} %shard_map.46) | data formatting | bytes 1572864
Async XLA Ops:
  0.0 0.7 %copy-start = (s32[144]{0:T(256)S(1)}, s32[144]{0:T(256)}, u32[]{:S(2)}) copy-start(s32[144]{0:T(256)} %param.5) | copy-start | bytes 1732
  0.7 0.7 %copy-start.1 = (s32[1,3]{1,0:T(1,128)S(1)}, s32[1,3]{1,0:T(1,128)}, u32[]{:S(2)}) copy-start(s32[1,3]{1,0:T(1,128)} %partner_hbm.1) | copy-start | bytes 40

commit v2 on v1

--- a/solution.py
+++ b/solution.py
@@ -200,7 +200,9 @@
     def normalize(inverse, chosen):
         for block in chosen:
             columns = slice(block * RB, (block + 1) * RB)
-            norm[:, columns] = (raw_ref[:, columns] * inverse[:, block : block + 1]).astype(
+            rows = slice(block * RB // HOP * stations, (block * RB // HOP + 1) * stations)
+            place = slice(block * RB % HOP, block * RB % HOP + RB)
+            norm[rows, place] = (raw_ref[:, columns] * inverse[:, block : block + 1]).astype(
                 jnp.bfloat16
             )
 
@@ -310,9 +312,8 @@
             for index in range(count):
                 other[slot, index] = expand(gathers[half][chosen, index], right_hot)
 
-            @pl.loop(0, bins // tile)
-            def _(step):
-                rows = pl.ds(pl.multiple_of(step * tile, tile), tile)
+            for step in range(bins // tile):
+                rows = slice(step * tile, (step + 1) * tile)
                 if half == 0:
                     real_sum = jnp.zeros((tile, pairs), jnp.float32)
                     imag_sum = jnp.zeros((tile, pairs), jnp.float32)
@@ -340,23 +341,23 @@
     for part in range(CHUNKS):
         columns = slice(part * CHUNK, (part + 1) * CHUNK)
         fetches[0][part].wait()
-        opening = dot(norm[:, HOP:], table[0, part])
+        fetches[1][part].wait()
+        opening = dot(norm[stations:], table[0, part])
+        closing = dot(norm[:stations], table[1, part])
         far_out[part] = opening[near_rows:].astype(jnp.bfloat16)
+        near_out[part] = closing[:near_rows].astype(jnp.bfloat16)
         keep[:near_rows, columns] = opening[:near_rows]
+        keep[near_rows:, columns] = closing[near_rows:]
         far_copies.append(remote(far_out.at[part], far_in.at[part], hop_send, hop_recv, part, up))
-        pl.when(has_next)(far_copies[-1].start)
-        fetches[1][part].wait()
-        closing = dot(norm[:, :HOP], table[1, part])
-        near_out[part] = closing[:near_rows].astype(jnp.bfloat16)
-        keep[near_rows:, columns] = closing[near_rows:]
         near_copies.append(
             remote(near_out.at[part], near_in.at[part], hop_send, hop_recv, CHUNKS + part, down)
         )
+        pl.when(has_next)(far_copies[-1].start)
         pl.when(has_prev)(near_copies[-1].start)
 
     for part in range(CHUNKS):
         columns = slice(part * CHUNK, (part + 1) * CHUNK)
-        own[:, columns] = dot(norm[:, :HOP], table[0, part]) + dot(norm[:, HOP:], table[1, part])
+        own[:, columns] = dot(norm[:stations], table[0, part]) + dot(norm[stations:], table[1, part])
     mixes = put_beams((0,), own[...], member)
 
     @pl.when(has_next)
@@ -446,7 +447,7 @@
             pltpu.VMEM((NBIN, NBIN), jnp.bfloat16),
             pltpu.VMEM((2 * PAD + blocks, wide), jnp.float32),
             pltpu.VMEM((2, PAD, wide), jnp.float32),
-            pltpu.VMEM((stations, samples), jnp.bfloat16),
+            pltpu.VMEM((2 * stations, HOP), jnp.bfloat16),
             pltpu.VMEM((stations, 2 * NBIN), jnp.float32),
             pltpu.VMEM((stations, 2 * NBIN), jnp.float32),
             pltpu.VMEM((CHUNKS, near_rows, CHUNK), jnp.bfloat16),
@@ -476,7 +477,7 @@
         compiler_params=pltpu.CompilerParams(
             collective_id=0, has_side_effects=True, vmem_limit_bytes=VMEM_BYTES
         ),
-    )(raw_data, station_group[None, :], partner_blocks, dft_table())
+    )(raw_data, pltpu.with_memory_space_constraint(station_group[None, :], pltpu.HBM), pltpu.with_memory_space_constraint(partner_blocks, pltpu.HBM), dft_table())
 
 
 def solution(mesh):

time: 27.5 us -> 25.8 us (0.938)
  local copies, waits for them, and re-layouts: 2.22 us -> 0.88 us
  Pallas kernels: 25.1 us -> 24.7 us
    unnamed x5 -> x1, local copies, waits for them, and re-layouts: 2.22 us -> 0.88 us
    pallas_call x1, Pallas kernels: 25.1 us -> 24.7 us  [body(): pl.pallas_call(functools.partial(spectra_kernel, slabs, groups, near_rows...]
where the time goes in v2:
time: 25.8 us; the launch traced here: 25.6 us
  Pallas kernels  24.7 us (96%)
  local copies, waits for them, and re-layouts  0.88 us (3%)
    pallas_call x1, Pallas kernels, body(): pl.pallas_call(functools.partial(spectra_kernel, slabs, groups, near_rows...  24.7 us
    unnamed x1, local copies, waits for them, and re-layouts  0.88 us

profile of v2, /device:TPU:0, one launch (start us, length us, event | category | flops | bytes accessed | tf_op | source)
XLA Modules:
  0.0 25.6 jit_solution(12827437739835823860)
XLA Ops:
  0.0 24.7 %shard_map.46 = f32[1,3,128,512]{3,2,1,0:T(8,128)S(1)} custom-call(f32[144,4096]{1,0:T(8,128)} %raw_hbm.1, s32[1,144]{1,0:T(1,128)} %bitcast.1, s32[1,3]{1,0:T(1,128)} %partner_hbm.1, bf16[2,4,2048,256]{3,2,1,0:T(8,128)(2,1)} %constant.2.clone.table_hbm), custom_call_target="tpu_custom_call" | custom-call | tf_op jit(solution)/shard_map/pallas_call | solution.py:437
  24.7 0.9 %copy.6 = f32[1,3,128,512]{3,2,1,0:T(8,128)} copy(f32[1,3,128,512]{3,2,1,0:T(8,128)S(1)} %shard_map.46) | data formatting | bytes 1572864

commit v3 on v2

--- a/solution.py
+++ b/solution.py
@@ -131,11 +131,6 @@
         pltpu.make_async_copy(group_hbm, group_ref, argument_sem.at[0]),
         pltpu.make_async_copy(partner_hbm, partner_ref, argument_sem.at[1]),
     )
-    for load in argument_loads:
-        load.start()
-    for part in range(CHUNKS):
-        for side in range(2):
-            fetches[side][part].start()
 
     barrier = pltpu.get_barrier_semaphore()
     for step in range(1, slabs):
@@ -153,6 +148,9 @@
     for block in range(blocks):
         if block * RB % chunk == 0:
             loads[block * RB // chunk].wait()
+            if block * RB // chunk == len(loads) - 1:
+                for copy in [*(fetches[at % 2][at // 2] for at in range(2 * CHUNKS)), *argument_loads]:
+                    copy.start()
         part = jnp.sum(jnp.abs(raw_ref[:, block * RB : (block + 1) * RB]), axis=1, keepdims=True)
         acc = jnp.where(lane == block, part, acc)
     tall = jnp.concatenate([acc, jnp.zeros((wide - stations, LANES), jnp.float32)], axis=0)

time: 25.8 us -> 23.8 us (0.922)
  Pallas kernels: 24.7 us -> 22.8 us
    pallas_call x1, Pallas kernels: 24.7 us -> 22.8 us  [body(): pl.pallas_call(functools.partial(spectra_kernel, slabs, groups, near_rows...]
where the time goes in v3:
time: 23.8 us; the launch traced here: 23.7 us
  Pallas kernels  22.8 us (96%)
  local copies, waits for them, and re-layouts  0.88 us (4%)
    pallas_call x1, Pallas kernels, body(): pl.pallas_call(functools.partial(spectra_kernel, slabs, groups, near_rows...  22.8 us
    unnamed x1, local copies, waits for them, and re-layouts  0.88 us

profile of v3, /device:TPU:0, one launch (start us, length us, event | category | flops | bytes accessed | tf_op | source)
XLA Modules:
  0.0 23.7 jit_solution(5361768648444731522)
XLA Ops:
  0.0 22.8 %shard_map.46 = f32[1,3,128,512]{3,2,1,0:T(8,128)S(1)} custom-call(f32[144,4096]{1,0:T(8,128)} %raw_hbm.1, s32[1,144]{1,0:T(1,128)} %bitcast.1, s32[1,3]{1,0:T(1,128)} %partner_hbm.1, bf16[2,4,2048,256]{3,2,1,0:T(8,128)(2,1)} %constant.2.clone.table_hbm), custom_call_target="tpu_custom_call" | custom-call | tf_op jit(solution)/shard_map/pallas_call | solution.py:435
  22.8 0.9 %copy.6 = f32[1,3,128,512]{3,2,1,0:T(8,128)} copy(f32[1,3,128,512]{3,2,1,0:T(8,128)S(1)} %shard_map.46) | data formatting | bytes 1572864

commit v4 on v3

--- a/solution.py
+++ b/solution.py
@@ -71,6 +71,7 @@
     table,
     nearby,
     sums,
+    edge_out,
     halo,
     norm,
     own,
@@ -109,10 +110,11 @@
     nxt = jnp.minimum(t + 1, slabs - 1)
     prv = jnp.maximum(t - 1, 0)
 
-    chunk = samples // 4
+    edge, middle = RAMH, blocks - RAMH
+    spans = (range(edge), range(middle, blocks), range(edge, middle))
     loads = []
-    for part in range(4):
-        columns = slice(part * chunk, (part + 1) * chunk)
+    for part, span in enumerate(spans):
+        columns = slice(span[0] * RB, (span[-1] + 1) * RB)
         load = pltpu.make_async_copy(
             raw_hbm.at[:, columns], raw_ref.at[:, columns], raw_sem.at[part]
         )
@@ -144,19 +146,27 @@
 
     wide = sums.shape[1]
     lane = lax.broadcasted_iota(jnp.int32, (stations, LANES), 1)
-    acc = jnp.zeros((stations, LANES), jnp.float32)
-    for block in range(blocks):
-        if block * RB % chunk == 0:
-            loads[block * RB // chunk].wait()
-            if block * RB // chunk == len(loads) - 1:
-                for copy in [*(fetches[at % 2][at // 2] for at in range(2 * CHUNKS)), *argument_loads]:
-                    copy.start()
-        part = jnp.sum(jnp.abs(raw_ref[:, block * RB : (block + 1) * RB]), axis=1, keepdims=True)
-        acc = jnp.where(lane == block, part, acc)
-    tall = jnp.concatenate([acc, jnp.zeros((wide - stations, LANES), jnp.float32)], axis=0)
-    sums[0:PAD, :] = jnp.zeros((PAD, wide), jnp.float32)
-    sums[PAD : PAD + blocks, :] = tall.T[:blocks, :]
-    sums[PAD + blocks : 2 * PAD + blocks, :] = jnp.zeros((PAD, wide), jnp.float32)
+    def add_sums(acc, span):
+        for block in span:
+            columns = slice(block * RB, (block + 1) * RB)
+            part = jnp.sum(jnp.abs(raw_ref[:, columns]), axis=1, keepdims=True)
+            acc = jnp.where(lane == block, part, acc)
+        return acc
+
+    def by_block(acc):
+        tall = jnp.concatenate([acc, jnp.zeros((wide - stations, LANES), jnp.float32)], axis=0)
+        return tall.T[:blocks, :]
+
+    loads[0].wait()
+    acc = add_sums(jnp.zeros((stations, LANES), jnp.float32), spans[0])
+    for load in loads[1:]:
+        load.wait()
+    for copy in [*(fetches[at % 2][at // 2] for at in range(2 * CHUNKS)), *argument_loads]:
+        copy.start()
+    acc = add_sums(acc, spans[1])
+    ends = by_block(acc)
+    edge_out[0] = ends[blocks - PAD :]
+    edge_out[1] = ends[:PAD]
 
     pl.semaphore_wait(barrier, slabs - 1 + groups - 1)
 
@@ -172,8 +182,8 @@
 
     up = {"tchunk": nxt}
     down = {"tchunk": prv}
-    sums_up = remote(sums.at[blocks : blocks + PAD, :], halo.at[0], sum_send, sum_recv, 0, up)
-    sums_down = remote(sums.at[PAD : 2 * PAD, :], halo.at[1], sum_send, sum_recv, 1, down)
+    sums_up = remote(edge_out.at[0], halo.at[0], sum_send, sum_recv, 0, up)
+    sums_down = remote(edge_out.at[1], halo.at[1], sum_send, sum_recv, 1, down)
 
     @pl.when(has_next)
     def _():
@@ -182,6 +192,10 @@
     @pl.when(has_prev)
     def _():
         sums_down.start()
+
+    sums[0:PAD, :] = jnp.zeros((PAD, wide), jnp.float32)
+    sums[PAD : PAD + blocks, :] = by_block(add_sums(acc, spans[2]))
+    sums[PAD + blocks : 2 * PAD + blocks, :] = jnp.zeros((PAD, wide), jnp.float32)
 
     def inverses():
         window = sums[PAD - RAMH : PAD - RAMH + blocks, :]
@@ -424,7 +438,7 @@
     groups = lax.axis_size("stn")
     bins = NBIN // slabs
     blocks = samples // RB
-    near_rows = -(-stations // 32) * 16
+    near_rows = -(-stations // 16) * 8
     wide = -(-stations // LANES) * LANES
     vmem = pl.BlockSpec(memory_space=pltpu.VMEM)
     dma = pltpu.SemaphoreType.DMA
@@ -445,6 +459,7 @@
             pltpu.VMEM((NBIN, NBIN), jnp.bfloat16),
             pltpu.VMEM((2 * PAD + blocks, wide), jnp.float32),
             pltpu.VMEM((2, PAD, wide), jnp.float32),
+            pltpu.VMEM((2, PAD, wide), jnp.float32),
             pltpu.VMEM((2 * stations, HOP), jnp.bfloat16),
             pltpu.VMEM((stations, 2 * NBIN), jnp.float32),
             pltpu.VMEM((stations, 2 * NBIN), jnp.float32),
@@ -460,7 +475,7 @@
             pltpu.VMEM((groups,) + split_shape, jnp.bfloat16),
             pltpu.VMEM((2 * slabs, bins, pairs), jnp.float32),
             pltpu.VMEM((MAXP, 2 * slabs, bins, pairs), jnp.float32),
-            dma((4,)),
+            dma((3,)),
             dma((2, CHUNKS)),
             dma((2,)),
             dma((2,)),

time: 23.8 us -> 23.8 us (level)
  no operation moved by 1% of the time
where the time goes in v4:
time: 23.8 us; the launch traced here: 23.6 us
  Pallas kernels  22.8 us (96%)
  local copies, waits for them, and re-layouts  0.88 us (4%)
    pallas_call x1, Pallas kernels, body(): pl.pallas_call(functools.partial(spectra_kernel, slabs, groups, near_rows...  22.8 us
    unnamed x1, local copies, waits for them, and re-layouts  0.88 us

profile of v4, /device:TPU:0, one launch (start us, length us, event | category | flops | bytes accessed | tf_op | source)
XLA Modules:
  0.0 23.6 jit_solution(2074481134071690808)
XLA Ops:
  0.0 22.8 %shard_map.46 = f32[1,3,128,512]{3,2,1,0:T(8,128)S(1)} custom-call(f32[144,4096]{1,0:T(8,128)} %raw_hbm.1, s32[1,144]{1,0:T(1,128)} %bitcast.1, s32[1,3]{1,0:T(1,128)} %partner_hbm.1, bf16[2,4,2048,256]{3,2,1,0:T(8,128)(2,1)} %constant.2.clone.table_hbm), custom_call_target="tpu_custom_call" | custom-call | tf_op jit(solution)/shard_map/pallas_call | solution.py:449
  22.8 0.9 %copy.6 = f32[1,3,128,512]{3,2,1,0:T(8,128)} copy(f32[1,3,128,512]{3,2,1,0:T(8,128)S(1)} %shard_map.46) | data formatting | bytes 1572864

commit v5 on v4

--- a/solution.py
+++ b/solution.py
@@ -161,7 +161,7 @@
     acc = add_sums(jnp.zeros((stations, LANES), jnp.float32), spans[0])
     for load in loads[1:]:
         load.wait()
-    for copy in [*(fetches[at % 2][at // 2] for at in range(2 * CHUNKS)), *argument_loads]:
+    for copy in [*argument_loads, *(fetches[at % 2][at // 2] for at in range(2 * CHUNKS))]:
         copy.start()
     acc = add_sums(acc, spans[1])
     ends = by_block(acc)
@@ -198,9 +198,19 @@
     sums[PAD + blocks : 2 * PAD + blocks, :] = jnp.zeros((PAD, wide), jnp.float32)
 
     def inverses():
-        window = sums[PAD - RAMH : PAD - RAMH + blocks, :]
-        for offset in range(1, 2 * RAMH):
-            window = window + sums[PAD - RAMH + offset : PAD - RAMH + offset + blocks, :]
+        rows = blocks + 2 * RAMH - 2
+        total = sums[PAD - RAMH : PAD - RAMH + rows, :] + sums[PAD - RAMH + 1 : PAD - RAMH + rows + 1, :]
+        window = None
+        count, begin = 2, 0
+        while True:
+            if 2 * RAMH & count:
+                piece = total[begin : begin + blocks]
+                window = piece if window is None else window + piece
+                begin += count
+            if 2 * count > 2 * RAMH:
+                break
+            total = total[: total.shape[0] - count] + total[count:]
+            count *= 2
         here = t * blocks + lax.broadcasted_iota(jnp.int32, (blocks, wide), 0)
         counted = jnp.minimum(here + RAMH, blocks * slabs) - jnp.maximum(here - RAMH, 0)
         running = window / (RB * counted.astype(jnp.float32))
@@ -229,18 +239,6 @@
     def _():
         near_in[...] = jnp.zeros_like(near_in)
 
-    @pl.when(has_prev)
-    def _():
-        sums_up.wait_recv()
-        sums[0:PAD, :] = halo[0]
-
-    @pl.when(has_next)
-    def _():
-        sums_down.wait_recv()
-        sums[PAD + blocks : 2 * PAD + blocks, :] = halo[1]
-
-    normalize(inverses(), [*range(first), *range(last, blocks)])
-
     row = lax.broadcasted_iota(jnp.int32, (NBIN, NBIN), 0)
     col = lax.broadcasted_iota(jnp.int32, (NBIN, NBIN), 1)
     nearby[...] = (jnp.abs(row - col) <= SMOOTH).astype(jnp.float32).astype(jnp.bfloat16)
@@ -249,6 +247,18 @@
     member = (
         group_ref[...] == lax.broadcasted_iota(jnp.int32, (SUB, stations), 0)
     ).astype(jnp.float32)
+
+    @pl.when(has_prev)
+    def _():
+        sums_up.wait_recv()
+        sums[0:PAD, :] = halo[0]
+
+    @pl.when(has_next)
+    def _():
+        sums_down.wait_recv()
+        sums[PAD + blocks : 2 * PAD + blocks, :] = halo[1]
+
+    normalize(inverses(), [*range(first), *range(last, blocks)])
 
     def put_beams(pieces, spectra, members):
         sums_here = jnp.dot(

time: 23.8 us -> 23.7 us (level)
  no operation moved by 1% of the time
where the time goes in v5:
time: 23.7 us; the launch traced here: 23.5 us
  Pallas kernels  22.7 us (96%)
  local copies, waits for them, and re-layouts  0.88 us (4%)
    pallas_call x1, Pallas kernels, body(): pl.pallas_call(functools.partial(spectra_kernel, slabs, groups, near_rows...  22.7 us
    unnamed x1, local copies, waits for them, and re-layouts  0.88 us

profile of v5, /device:TPU:0, one launch (start us, length us, event | category | flops | bytes accessed | tf_op | source)
XLA Modules:
  0.0 23.5 jit_solution(9901720277931506360)
XLA Ops:
  0.0 22.7 %shard_map.46 = f32[1,3,128,512]{3,2,1,0:T(8,128)S(1)} custom-call(f32[144,4096]{1,0:T(8,128)} %raw_hbm.1, s32[1,144]{1,0:T(1,128)} %bitcast.1, s32[1,3]{1,0:T(1,128)} %partner_hbm.1, bf16[2,4,2048,256]{3,2,1,0:T(8,128)(2,1)} %constant.2.clone.table_hbm), custom_call_target="tpu_custom_call" | custom-call | tf_op jit(solution)/shard_map/pallas_call | solution.py:459
  22.7 0.9 %copy.6 = f32[1,3,128,512]{3,2,1,0:T(8,128)} copy(f32[1,3,128,512]{3,2,1,0:T(8,128)S(1)} %shard_map.46) | data formatting | bytes 1572864
